TPU v7x, 512 devices: a whole 4x4x16 slice. The times are simulated.
512 devices in a mesh: req: 128 (over x, z, core), tp: 4 (over y).
Axes of the slice: x: 4, y: 4, z: 16, core: 2. Of those that a mesh axis runs over, the one named last changes fastest.
Arguments:
- queries: bfloat16 [2, 128, 32, 1536], P(None, 'req', None, 'tp')
- response_kv: bfloat16 [2, 128, 2, 32, 256], P(None, 'req'), may hold values from -6 to 6
- cache_kv: bfloat16 [2, 128, 2, 384, 256], P(None, 'req'), may hold values from -6 to 6
- residual: bfloat16 [2, 128, 32, 1536], P(None, 'req')
- out_proj: bfloat16 [2, 1536, 1536], P(None, 'tp'), may hold values from -0.5 to 0.5
- norm_gain: float32 [2, 1536], replicated, may hold values from 0.25 to 1.75
- lm_head: bfloat16 [2, 131072, 1536], P(None, 'req', 'tp')
- targets: int32 [128, 32], P(None, 'tp'), may hold values from 0 to 131071
- resp_lengths: int32 [128], replicated, may hold values from 1 to 32, 2560 in all
- cache_lengths: int32 [128], P('req'), may hold values from 1 to 384, 30720 in all
- owner_slot: int32 [128], replicated, may hold values from 0 to 127, each once
- sink_count: int32 [1], replicated, may hold values from 1 to 95
- window_size: int32 [1], replicated, may hold values from 48 to 191
Outputs:
- token_logprobs: float32 [128, 32], P('req', 'tp')
- request_scores: float32 [128, 2], P('req')
Inputs may be any that keep to these rules, and one draw needn't show every extreme that they name: `resp_lengths`: live response slots are the first ones; all lengths sum to 2560. `cache_lengths`: live cache slots are the first ones; all lengths sum to 30720. `owner_slot`: A permutation of the requests.
All inputs are finite; a program needn't handle non-finite values. No bound on the sum of `cache_lengths` on one device may be relied on, other than what follows from the above.
Results may differ from a plain program's by a relative error of at most 0.0014.
Values may be sent and summed in bfloat16 or wider, within the bound.
A program may use at most 128 MiB of HBM per device.

v0:
```python
import jax
import jax.numpy as jnp
from jax import lax
from jax.sharding import PartitionSpec as P

HEADS = 12
HEAD = 128
KV_HEADS = 2
RESP = 32
CACHE = 384


def span_mask(lengths, sink_count, window_size):
    cache_pos = jnp.arange(CACHE, dtype=jnp.int32)
    slot_pos = jnp.arange(RESP, dtype=jnp.int32)
    req_count = lengths.shape[0]
    key_pos = jnp.concatenate([cache_pos[None, :], lengths[:, None] + slot_pos[None, :]], axis=1)
    key_live = jnp.concatenate(
        [cache_pos[None, :] < lengths[:, None], jnp.ones((req_count, RESP), jnp.bool_)], axis=1
    )
    query_pos = lengths[:, None] + slot_pos[None, :]
    earlier = key_pos[:, None, :] <= query_pos[:, :, None]
    inside = (key_pos[:, None, :] < sink_count[0]) | (
        query_pos[:, :, None] - key_pos[:, None, :] < window_size[0]
    )
    return key_live[:, None, :] & earlier & inside


def rms_norm(hidden, norm_gain):
    scale_inv = lax.rsqrt(jnp.mean(hidden * hidden, axis=-1, keepdims=True) + 1e-06)
    return (hidden * scale_inv * norm_gain[:, None, None, :]).astype(jnp.bfloat16)


def per_device(
    queries,
    response_kv,
    cache_kv,
    residual,
    out_proj,
    norm_gain,
    lm_head,
    targets,
    resp_lengths,
    cache_lengths,
    owner_slot,
    sink_count,
    window_size,
):
    tp_size = lax.axis_size("tp")
    tp_index = lax.axis_index("tp")
    req_index = lax.axis_index("req")
    local_reqs = queries.shape[1]
    local_heads = HEADS // tp_size
    group_size = HEADS // KV_HEADS
    kv_index = tp_index * local_heads // group_size
    quarter = RESP // tp_size
    cache_head = lax.dynamic_slice_in_dim(cache_kv, kv_index * HEAD, HEAD, axis=4)
    resp_head = lax.dynamic_slice_in_dim(response_kv, kv_index * HEAD, HEAD, axis=4)
    key_rows = jnp.concatenate([cache_head[:, :, 0], resp_head[:, :, 0]], axis=2)
    value_rows = jnp.concatenate([cache_head[:, :, 1], resp_head[:, :, 1]], axis=2)
    query_heads = queries.reshape(2, local_reqs, RESP, local_heads, HEAD)
    scores = jnp.einsum(
        "mrshd,mrkd->mrhsk", query_heads, key_rows, preferred_element_type=jnp.float32
    ) * HEAD ** (-0.5)
    allowed = span_mask(cache_lengths, sink_count, window_size)[None, :, None]
    masked = jnp.where(allowed, scores, -jnp.inf)
    row_peak = jnp.max(masked, axis=-1, keepdims=True)
    weights = jnp.exp(masked - row_peak)
    weights = (weights / jnp.sum(weights, axis=-1, keepdims=True)).astype(jnp.bfloat16)
    attended = jnp.einsum(
        "mrhsk,mrkd->mrshd", weights, value_rows, preferred_element_type=jnp.float32
    )
    attended = attended.astype(jnp.bfloat16).reshape(2, local_reqs, RESP, local_heads * HEAD)
    partial_value = jnp.einsum(
        "mrsf,mfd->mrsd", attended, out_proj, preferred_element_type=jnp.float32
    )
    start_slot = tp_index * quarter
    projected = lax.dynamic_slice_in_dim(lax.psum(partial_value, "tp"), start_slot, quarter, axis=2)
    own_residual = lax.dynamic_slice_in_dim(residual, start_slot, quarter, axis=2)
    hidden = own_residual.astype(jnp.float32) + projected
    normed = rms_norm(hidden, norm_gain)
    flat_rows = normed.reshape(2, local_reqs * quarter, normed.shape[3])
    full_head = lax.all_gather(lm_head, "tp", axis=2, tiled=True)
    vocab_rows = full_head.shape[1]
    vocab_start = req_index * vocab_rows
    flat_targets = targets.reshape(-1)
    total_rows = flat_targets.shape[0]
    requests = total_rows // quarter
    logits = jnp.einsum(
        "mnd,mvd->mnv",
        lax.all_gather(flat_rows, "req", axis=1, tiled=True),
        full_head,
        preferred_element_type=jnp.float32,
    )
    block_peak = jnp.max(logits, axis=-1)
    block_total = jnp.sum(jnp.exp(logits - block_peak[..., None]), axis=-1)
    wanted = flat_targets - vocab_start
    target_hits = jnp.arange(vocab_rows, dtype=jnp.int32)[None, None, :] == wanted[None, :, None]
    block_pick = jnp.sum(jnp.where(target_hits, logits, 0.0), axis=-1)
    peak_all = block_peak
    total_all = block_total
    picked_all = block_pick
    peak_all = peak_all.reshape(2, requests, quarter)
    total_all = total_all.reshape(2, requests, quarter)
    picked_all = picked_all.reshape(2, requests, quarter)
    row_order = (
        jnp.zeros((requests,), jnp.int32).at[owner_slot].set(jnp.arange(requests, dtype=jnp.int32))
    )
    owned_reqs = lax.dynamic_slice_in_dim(row_order, req_index * local_reqs, local_reqs)
    vocab_top = lax.pmax(peak_all, "req")
    exp_total, picked = lax.psum((total_all * jnp.exp(peak_all - vocab_top), picked_all), "req")
    logprob = (picked - (vocab_top + jnp.log(exp_total)))[:, owned_reqs]
    lengths_owned = resp_lengths[owned_reqs]
    live_slots = (start_slot + jnp.arange(quarter, dtype=jnp.int32))[None, :] < lengths_owned[
        :, None
    ]
    policy = jnp.where(live_slots, logprob[0], 0.0)
    log_ratio = jnp.where(live_slots, logprob[0] - logprob[1], 0.0)
    policy_total, ratio_total = lax.psum(
        (jnp.sum(policy, axis=1), jnp.sum(log_ratio, axis=1)), "tp"
    )
    counts = lengths_owned.astype(jnp.float32)
    request_scores = jnp.stack([policy_total / counts, ratio_total / counts], axis=1)
    return (policy, request_scores)


def solution(mesh):
    in_specs = (
        P(None, "req", None, "tp"),
        P(None, "req", None, None, None),
        P(None, "req", None, None, None),
        P(None, "req", None, None),
        P(None, "tp", None),
        P(),
        P(None, "req", "tp"),
        P(None, "tp"),
        P(),
        P("req"),
        P(),
        P(),
        P(),
    )
    out_specs = (P("req", "tp"), P("req", None))
    return jax.shard_map(
        per_device, mesh=mesh, in_specs=in_specs, out_specs=out_specs, check_vma=False
    )
```

profile of v0, /device:TPU:8, one launch (start us, length us, event | category | flops | bytes accessed | tf_op | source)
XLA Modules:
  0.0 1325.8 jit_solution(16412632593061100903)
XLA Ops:
  7.2 0.0 copy-start
  7.2 0.0 copy-start.1
  7.2 0.0 copy-start.2
  7.2 0.0 copy-start.3
  7.2 0.0 copy-start.4
  7.2 0.0 copy-start.5
  7.2 0.0 all-reduce.5.cloned.1.call-start
  7.3 1.2 dynamic-slice_bitcast_fusion
  8.5 0.8 dynamic-slice_bitcast_fusion.2
  11.3 0.8 reshape.303
  12.1 0.1 fusion.12
  12.2 0.3 fusion.23
  12.6 0.2 fusion.5
  12.8 0.3 fusion.4
  13.1 0.1 reshape.305
  13.2 0.0 copy-done
  13.2 1.3 convolution_bitcast_fusion
  14.4 0.0 all-reduce.5.cloned.1.call-update
  14.4 0.0 all-gather.4.cloned.1.call-start
  14.5 0.7 all-gather.4.cloned.1.call-update
  15.2 0.0 all-gather.6.cloned.1.call-start
  15.3 60.6 %all-reduce.5.cloned.1.call-done = f32[2,1,32,1536]{3,2,0,1:T(8,128)} async-done(((f32[2,1,32,1536]{3,2,0,1:T(8,128)}), f32[2,1,32,1536]{3,2,0,1:T(8,128)}) %all-reduce.5.cloned.1.call-update) | async-done | bytes 393232 | tf_op jit(solution)/shard_map/psum | solution.py:78
  75.8 0.0 copy-done.1
  75.8 1.0 multiply_reduce_fusion
  76.8 0.0 copy-done.2
  76.9 1.6 multiply_convert_fusion
  78.4 0.0 all-gather.6.cloned.1.call-update
  78.5 0.0 copy-done.3
  78.5 0.1 copy.19
  78.6 0.1 sub.65
  78.7 0.0 copy-done.4
  78.7 1.0 scatter_custom_fusion
  79.7 0.6 dynamic_slice.15
  82.2 0.0 copy-done.5
  82.2 0.6 dynamic-slice.5
  83.5 0.8 iota_compare_fusion
  84.3 68.4 %all-gather.4.cloned.1.call-done = bf16[2,1024,1536]{2,1,0:T(8,128)(2,1)} async-done(((bf16[2,1024,384]{2,1,0:T(8,128)(2,1)}), bf16[2,1024,1536]{2,1,0:T(8,128)(2,1)}) %all-gather.4.cloned.1.call-update) | async-done | bytes 6291472 | tf_op jit(solution)/shard_map/all_gather | solution.py:83
  152.7 149.5 %all-gather.6.cloned.1.call-done = bf16[2,1,1024,1536]{3,2,0,1:T(8,128)(2,1)} async-done(((bf16[2,1,8,1536]{3,2,0,1:T(8,128)(2,1)}), bf16[2,1,1024,1536]{3,2,0,1:T(8,128)(2,1)}) %all-gather.6.cloned.1.call-update) | async-done | bytes 6291472 | tf_op jit(solution)/shard_map/all_gather | solution.py:91
  302.2 12.7 fusion.24
  314.9 0.1 reshape.308
  315.0 5.1 exponential_reduce_fusion
  320.1 0.8 reshape.309
  320.9 493.2 %pmax.7 = f32[2,128,8]{2,1,0:T(8,128)S(1)} all-reduce(f32[2,128,8]{2,1,0:T(8,128)S(1)} %reshape.308), channel_id=1, replica_groups=mesh['req'=128,'tp'=4] {'req'}, use_global_device_ids=true, to_apply=%region_8.9 | all-reduce | flops 2048 | bytes 16384 | tf_op jit(solution)/shard_map/pmax | solution.py:110
  814.1 0.1 reshape.307
  814.2 490.9 %all-reduce.1 = (f32[2,128,8]{2,1,0:T(8,128)S(1)}, f32[2,128,8]{2,1,0:T(8,128)S(1)}) all-reduce(f32[2,128,8]{2,1,0:T(8,128)S(1)} %reshape.307, f32[2,128,8]{2,1,0:T(8,128)S(1)} %exponential_multiply_fusion), channel_id=1, replica_groups=mesh['req'=128,'tp'=4] {'req'}, use_global_device_ids=true, to_apply=%region_6.7 | all-reduce | flops 4096 | bytes 32768 | tf_op jit(solution)/shard_map/psum | solution.py:111
  1305.2 1.2 fusion.17
  1306.4 1.7 fusion.22
  1308.1 9.3 all-reduce.2
  1318.7 0.6 pad_maximum_fusion
  (14 shorter events, 0.2 us)
Async XLA Ops:
  7.2 6.0 copy-start
  7.2 68.7 %copy-start.1 = (bf16[2,1,32,1536]{3,2,1,0:T(8,128)(2,1)S(1)}, bf16[2,1,32,1536]{3,2,1,0:T(8,128)(2,1)}, u32[]{:S(2)}) copy-start(bf16[2,1,32,1536]{3,2,1,0:T(8,128)(2,1)} %param.16) | copy-start | bytes 589828
  7.2 69.7 %copy-start.2 = (f32[2,1536]{1,0:T(2,128)S(1)}, f32[2,1536]{1,0:T(2,128)}, u32[]{:S(2)}) copy-start(f32[2,1536]{1,0:T(2,128)} %param.18) | copy-start | bytes 36868
  7.2 71.3 %copy-start.3 = (s32[128,8]{0,1:T(8,128)S(1)}, s32[128,8]{0,1:T(8,128)}, u32[]{:S(2)}) copy-start(s32[128,8]{0,1:T(8,128)} %param.20) | copy-start | bytes 12292
  7.2 71.5 %copy-start.4 = (s32[128]{0:T(128)S(1)}, s32[128]{0:T(128)}, u32[]{:S(2)}) copy-start(s32[128]{0:T(128)} %param.23) | copy-start | bytes 1540
  7.2 75.0 %copy-start.5 = (s32[128]{0:T(128)S(1)}, s32[128]{0:T(128)}, u32[]{:S(2)}) copy-start(s32[128]{0:T(128)} %param.21) | copy-start | bytes 1540
  7.2 68.6 %all-reduce.5.cloned.1.call-start = ((), (), s32[]{:S(2)}) async-start(), calls=%async_computation | async-start | bytes 786432 | tf_op jit(solution)/shard_map/psum | solution.py:78
  14.4 138.2 %all-gather.4.cloned.1.call-start = ((), (), s32[]{:S(2)}) async-start(), calls=%async_computation.1 | async-start | bytes 7864320 | tf_op jit(solution)/shard_map/all_gather | solution.py:83
  15.2 287.0 %all-gather.6.cloned.1.call-start = ((), (), s32[]{:S(2)}) async-start(), calls=%async_computation.2 | async-start | bytes 6340608 | tf_op jit(solution)/shard_map/all_gather | solution.py:91
Sparse Core Ops, SparseCore 0:
  14.6 61.2 all-reduce.4
  78.2 74.4 all-gather.3
  156.4 145.7 all-gather.5
where the time goes:
time: 1330 us
  blocking collectives  993 us (75%)
  waiting for transfers between devices  279 us (21%)
  between operations  19.9 us (1%)
  matrix products  14.6 us (1%)
    pmax x1, blocking collectives, per_device(): vocab_top = lax.pmax(peak_all, 'req')  493 us
    psum x1, blocking collectives, per_device(): lax.psum((total_all * jnp.exp(peak_all - vocab_top), picked_all), 'req')  491 us
    all_gather x1, waiting for transfers between devices, per_device(): lax.all_gather(flat_rows, 'req', axis=1, tiled=True)  149 us
    all_gather x1, waiting for transfers between devices, per_device(): full_head = lax.all_gather(lm_head, 'tp', axis=2, tiled=True)  68.4 us
    psum x1, waiting for transfers between devices, per_device(): lax.psum(partial_value, 'tp')  60.6 us
  transfers between devices with their start and end apart: 3, of which 3 were waited for; matrix products, arithmetic and copies ran while one was open for 0% of the time, Pallas kernels for 0%

commit v1 on v0

--- a/solution.py
+++ b/solution.py
@@ -8,6 +8,24 @@
 KV_HEADS = 2
 RESP = 32
 CACHE = 384
+
+
+def ring_gather(value, axis, dim):
+    ways, here, step = (lax.axis_size(axis), lax.axis_index(axis), value.shape[dim])
+    shape = [n * ways if d == dim else n for d, n in enumerate(value.shape)]
+    full = lax.dynamic_update_slice_in_dim(
+        jnp.zeros(shape, value.dtype), value, here * step, axis=dim
+    )
+    going_up = going_down = value
+    for far in range(1, ways // 2 + 1):
+        going_up = lax.ppermute(going_up, axis, [(d, (d + 1) % ways) for d in range(ways)])
+        full = lax.dynamic_update_slice_in_dim(full, going_up, (here - far) % ways * step, axis=dim)
+        if 2 * far < ways:
+            going_down = lax.ppermute(going_down, axis, [(d, (d - 1) % ways) for d in range(ways)])
+            full = lax.dynamic_update_slice_in_dim(
+                full, going_down, (here + far) % ways * step, axis=dim
+            )
+    return full
 
 
 def span_mask(lengths, sink_count, window_size):
@@ -80,7 +98,7 @@
     hidden = own_residual.astype(jnp.float32) + projected
     normed = rms_norm(hidden, norm_gain)
     flat_rows = normed.reshape(2, local_reqs * quarter, normed.shape[3])
-    full_head = lax.all_gather(lm_head, "tp", axis=2, tiled=True)
+    full_head = ring_gather(lm_head, "tp", 2)
     vocab_rows = full_head.shape[1]
     vocab_start = req_index * vocab_rows
     flat_targets = targets.reshape(-1)

time: 1330 us -> 1250 us (0.940)
  waiting for transfers between devices: 279 us -> 180 us
    all_gather x1, waiting for transfers between devices: 149 us -> 72 us  [per_device(): lax.all_gather(flat_rows, 'req', axis=1, tiled=True)]
    all_gather x1 -> x0, waiting for transfers between devices: 68.4 us -> none  [per_device(): full_head = lax.all_gather(lm_head, 'tp', axis=2, tiled=True)]
    ppermute x0 -> x3, waiting for transfers between devices: none -> 46.9 us  [the longest x2 46.9 us: ring_gather(): lax.ppermute(going_up, axis, [(d, (d + 1) % ways) for d in range(ways)])]
  transfers between devices with their start and end apart: 3 -> 5, of which waited for: 3 -> 4; matrix products, arithmetic and copies ran while one was open for 0% -> 1% of each run, Pallas kernels for 0% -> 0%
where the time goes in v1:
time: 1250 us
  blocking collectives  993 us (79%)
  waiting for transfers between devices  180 us (14%)
  between operations  20.3 us (2%)
  local copies, waits for them, and re-layouts  19.2 us (2%)
  matrix products  14.6 us (1%)
    pmax x1, blocking collectives, per_device(): vocab_top = lax.pmax(peak_all, 'req')  493 us
    psum x1, blocking collectives, per_device(): lax.psum((total_all * jnp.exp(peak_all - vocab_top), picked_all), 'req')  491 us
    all_gather x1, waiting for transfers between devices, per_device(): lax.all_gather(flat_rows, 'req', axis=1, tiled=True)  72 us
    psum x1, waiting for transfers between devices, per_device(): lax.psum(partial_value, 'tp')  61.3 us
    ppermute x2, waiting for transfers between devices, ring_gather(): lax.ppermute(going_up, axis, [(d, (d + 1) % ways) for d in range(ways)])  46.9 us
  transfers between devices with their start and end apart: 5, of which 4 were waited for; matrix products, arithmetic and copies ran while one was open for 1% of the time, Pallas kernels for 0%

profile of v1, /device:TPU:8, one launch (start us, length us, event | category | flops | bytes accessed | tf_op | source)
XLA Modules:
  0.0 1249.6 jit_solution(13006740128564873232)
XLA Ops:
  7.2 0.0 copy-start
  7.2 0.0 copy-start.2
  7.2 0.0 copy-start.3
  7.2 0.0 copy-start.4
  7.2 0.0 copy-start.5
  7.2 0.0 copy-start.6
  7.2 0.0 all-reduce.5.cloned.1.call-start
  7.3 1.2 dynamic-slice_bitcast_fusion
  8.5 0.8 dynamic-slice_bitcast_fusion.2
  11.3 0.8 reshape.303
  12.1 0.1 fusion.12
  12.2 0.3 fusion.23
  12.6 0.2 fusion.5
  12.8 0.3 fusion.4
  13.1 0.1 reshape.305
  13.2 0.0 copy-done
  13.2 1.3 convolution_bitcast_fusion
  14.4 0.0 all-reduce.5.cloned.1.call-update
  14.4 0.0 all-gather.3.cloned.1.call-start
  14.5 61.3 %all-reduce.5.cloned.1.call-done = f32[2,1,32,1536]{3,2,0,1:T(8,128)} async-done(((f32[2,1,32,1536]{3,2,0,1:T(8,128)}), f32[2,1,32,1536]{3,2,0,1:T(8,128)}) %all-reduce.5.cloned.1.call-update) | async-done | bytes 393232 | tf_op jit(solution)/shard_map/psum | solution.py:96
  75.8 0.0 copy-done.2
  75.8 1.0 multiply_reduce_fusion
  76.8 0.0 copy-done.3
  76.8 1.6 multiply_convert_fusion
  78.4 0.0 all-gather.3.cloned.1.call-update
  78.4 3.5 collective-permute-start
  81.9 2.4 collective-permute-start.1
  84.3 30.4 %collective-permute-done = bf16[2,1024,384]{2,1,0:T(8,128)(2,1)} collective-permute-done((bf16[2,1024,384]{2,1,0:T(8,128)(2,1)}, bf16[2,1024,384]{2,1,0:T(8,128)(2,1)}, u32[]{:S(2)}, u32[]{:S(2)}) %collective-permute-start) | collective-permute-done | bytes 1572896 | tf_op jit(solution)/shard_map/ppermute | solution.py:21
  114.7 3.6 collective-permute-start.2
  118.4 0.0 copy-done.4
  118.4 0.1 copy.19
  118.5 0.1 sub.71
  118.6 0.0 copy-done.5
  118.6 1.0 scatter_custom_fusion
  119.6 0.6 dynamic_slice.15
  122.1 0.0 copy-done.6
  122.1 0.6 dynamic-slice.5
  123.4 0.0 copy-start.1
  123.4 3.0 broadcast_in_dim.41
  126.4 0.0 copy-done.1
  126.4 1.4 constant_dynamic-update-slice_fusion.3
  127.8 0.8 iota_compare_fusion
  128.6 2.8 constant_dynamic-update-slice_fusion.2
  131.4 0.0 collective-permute-done.1
  131.4 2.8 constant_dynamic-update-slice_fusion.1
  134.2 16.6 %collective-permute-done.2 = bf16[2,1024,384]{2,1,0:T(8,128)(2,1)} collective-permute-done((bf16[2,1024,384]{2,1,0:T(8,128)(2,1)}, bf16[2,1024,384]{2,1,0:T(8,128)(2,1)}, u32[]{:S(2)}, u32[]{:S(2)}) %collective-permute-start.2) | collective-permute-done | bytes 1572896 | tf_op jit(solution)/shard_map/ppermute | solution.py:21
  150.8 2.9 constant_dynamic-update-slice_fusion
  153.7 72.0 %all-gather.3.cloned.1.call-done = bf16[2,1,1024,1536]{3,2,0,1:T(8,128)(2,1)} async-done(((bf16[2,1,8,1536]{3,2,0,1:T(8,128)(2,1)}), bf16[2,1,1024,1536]{3,2,0,1:T(8,128)(2,1)}) %all-gather.3.cloned.1.call-update) | async-done | bytes 6291472 | tf_op jit(solution)/shard_map/all_gather | solution.py:109
  225.7 12.7 %fusion.24 = (f32[2,1024]{1,0:T(2,128)S(1)}, f32[2,1024,1024]{1,2,0:T(8,128)}) fusion(bf16[2,1024,1536]{2,1,0:T(8,128)(2,1)} %constant_dynamic-update-slice_fusion, bf16[2,1,1024,1536]{3,2,0,1:T(8,128)(2,1)} %all-gather.3.cloned.1.call-done), kind=kOutput, calls=%fused_computation.64 | convolution fusion | flops 6444546048 | bytes 20979712 | tf_op jit(solution)/shard_map/mnd,mvd->mnv/dot_general | solution.py:107
  238.4 0.1 reshape.308
  238.5 5.1 exponential_reduce_fusion
  243.6 0.8 reshape.309
  244.4 493.2 %pmax.7 = f32[2,128,8]{2,1,0:T(8,128)S(1)} all-reduce(f32[2,128,8]{2,1,0:T(8,128)S(1)} %reshape.308), channel_id=1, replica_groups=mesh['req'=128,'tp'=4] {'req'}, use_global_device_ids=true, to_apply=%region_8.9 | all-reduce | flops 2048 | bytes 16384 | tf_op jit(solution)/shard_map/pmax | solution.py:128
  737.6 0.1 reshape.307
  737.7 490.9 %all-reduce.1 = (f32[2,128,8]{2,1,0:T(8,128)S(1)}, f32[2,128,8]{2,1,0:T(8,128)S(1)}) all-reduce(f32[2,128,8]{2,1,0:T(8,128)S(1)} %reshape.307, f32[2,128,8]{2,1,0:T(8,128)S(1)} %exponential_multiply_fusion), channel_id=1, replica_groups=mesh['req'=128,'tp'=4] {'req'}, use_global_device_ids=true, to_apply=%region_6.7 | all-reduce | flops 4096 | bytes 32768 | tf_op jit(solution)/shard_map/psum | solution.py:129
  1228.6 1.2 fusion.17
  1229.8 1.7 fusion.22
  1231.6 9.3 all-reduce.2
  1242.2 0.6 pad_maximum_fusion
  (14 shorter events, 0.2 us)
Async XLA Ops:
  7.2 6.0 copy-start
  7.2 68.6 %copy-start.2 = (bf16[2,1,32,1536]{3,2,1,0:T(8,128)(2,1)S(1)}, bf16[2,1,32,1536]{3,2,1,0:T(8,128)(2,1)}, u32[]{:S(2)}) copy-start(bf16[2,1,32,1536]{3,2,1,0:T(8,128)(2,1)} %param.16) | copy-start | bytes 589828
  7.2 69.6 %copy-start.3 = (f32[2,1536]{1,0:T(2,128)S(1)}, f32[2,1536]{1,0:T(2,128)}, u32[]{:S(2)}) copy-start(f32[2,1536]{1,0:T(2,128)} %param.18) | copy-start | bytes 36868
  7.2 111.2 %copy-start.4 = (s32[128,8]{0,1:T(8,128)S(1)}, s32[128,8]{0,1:T(8,128)}, u32[]{:S(2)}) copy-start(s32[128,8]{0,1:T(8,128)} %param.20) | copy-start | bytes 12292
  7.2 111.4 %copy-start.5 = (s32[128]{0:T(128)S(1)}, s32[128]{0:T(128)}, u32[]{:S(2)}) copy-start(s32[128]{0:T(128)} %param.23) | copy-start | bytes 1540
  7.2 114.9 %copy-start.6 = (s32[128]{0:T(128)S(1)}, s32[128]{0:T(128)}, u32[]{:S(2)}) copy-start(s32[128]{0:T(128)} %param.21) | copy-start | bytes 1540
  7.2 68.6 %all-reduce.5.cloned.1.call-start = ((), (), s32[]{:S(2)}) async-start(), calls=%async_computation | async-start | bytes 786432 | tf_op jit(solution)/shard_map/psum | solution.py:96
  14.4 211.2 %all-gather.3.cloned.1.call-start = ((), (), s32[]{:S(2)}) async-start(), calls=%async_computation.1 | async-start | bytes 6340608 | tf_op jit(solution)/shard_map/all_gather | solution.py:109
  78.4 36.2 %collective-permute-start = (bf16[2,1024,384]{2,1,0:T(8,128)(2,1)}, bf16[2,1024,384]{2,1,0:T(8,128)(2,1)}, u32[]{:S(2)}, u32[]{:S(2)}) collective-permute-start(bf16[2,1024,384]{2,1,0:T(8,128)(2,1)} %param.19), channel_id=1, source_target_pairs={{0,1},{1,2},{2,3},{3,0},{4,5},{5,6},{6,7},{7,4},{8,9},{9,10},{10,1... | collective-permute-start | bytes 4718600 | tf_op jit(solution)/shard_map/ppermute | solution.py:21
  81.9 49.5 %collective-permute-start.1 = (bf16[2,1024,384]{2,1,0:T(8,128)(2,1)}, bf16[2,1024,384]{2,1,0:T(8,128)(2,1)}, u32[]{:S(2)}, u32[]{:S(2)}) collective-permute-start(bf16[2,1024,384]{2,1,0:T(8,128)(2,1)} %param.19), channel_id=1, source_target_pairs={{0,3},{1,0},{2,1},{3,2},{4,7},{5,4},{6,5},{7,6},{8,11},{9,8},{10,9... | collective-permute-start | bytes 4718600 | tf_op jit(solution)/shard_map/ppermute | solution.py:24
  114.7 36.1 %collective-permute-start.2 = (bf16[2,1024,384]{2,1,0:T(8,128)(2,1)}, bf16[2,1024,384]{2,1,0:T(8,128)(2,1)}, u32[]{:S(2)}, u32[]{:S(2)}) collective-permute-start(bf16[2,1024,384]{2,1,0:T(8,128)(2,1)} %collective-permute-done), channel_id=1, source_target_pairs={{0,1},{1,2},{2,3},{3,0},{4,5},{5,6},{6,7},{7,4},{8,9},{9,10},{10,1... | collective-permute-start | bytes 4718600 | tf_op jit(solution)/shard_map/ppermute | solution.py:21
  123.4 3.0 copy-start.1
Sparse Core Ops, SparseCore 0:
  14.6 61.1 all-reduce.4
  79.5 146.1 all-gather.2
